TPU v7x, 128 devices: a whole 4x4x4 slice. The times are simulated.
128 devices in a mesh: mod: 64 (over y, z, x), pair: 2 (over core).
Axes of the slice: x: 4, y: 4, z: 4, core: 2. Of those that a mesh axis runs over, the one named last changes fastest.
Arguments:
- query_grads: bfloat16 [512, 256, 16, 128], P(('mod', 'pair')), may hold values from -24 to 24
- train_grads: bfloat16 [1024, 256, 16, 128], P('pair', 'mod'), may hold values from -6 to 6
- left_basis: bfloat16 [256, 16, 16], P('mod'), may hold values from -1.5 to 1.5
- right_basis: bfloat16 [256, 128, 128], P('mod'), may hold values from -0.5 to 0.5
- eigenvalues: bfloat16 [256, 16, 128], P('mod'), may hold values from 0.0009994507 to 10
- block_rows: int32 [256], P('mod'), may hold values from 0 to 16, as said below
Outputs:
- scores: float32 [512, 1024], P('mod', 'pair')
Inputs may be any that keep to these rules, and one draw needn't show every extreme that they name: `block_rows`: owner j of the 64 owners holds slots j * 4 to (j + 1) * 4 - 1; of these the first 1 to 4 are live with 8 to 16 rows each and the rest hold 0; some owner has all 4 slots live and a slot of 16 rows, and some live slot has 8 rows.
All inputs are finite; a program needn't handle non-finite values.
Results may differ from a plain program's by a relative error of at most 0.0047.
Values may be sent and summed in bfloat16 or wider, within the bound.
No kernel may reach another device: no remote copies, remote signals or barrier semaphores. Data moves between devices by JAX's collectives and lax.ppermute only.
A program may use at most 128 MiB of HBM per device.

v0:
```python
import math

import jax
import jax.numpy as jnp
from jax import lax
from jax.sharding import PartitionSpec as P


def swapped(value, axis, stride):
    mask = 2**stride
    pairs = [(source, source ^ mask) for source in range(lax.axis_size(axis))]
    return lax.ppermute(value, axis, pairs)


def precondition(grad_slot, left_factor, right_factor, eig_block, live_rows):
    count_n, row_total, col_total = grad_slot.shape
    row_mask = (jnp.arange(row_total) < live_rows).astype(jnp.float32)
    left_masked = (left_factor.astype(jnp.float32) * row_mask[:, None] * row_mask[None, :]).astype(
        jnp.bfloat16
    )
    masked_grads = (grad_slot.astype(jnp.float32) * row_mask[None, :, None]).astype(jnp.bfloat16)
    rotated_right = (
        jnp.dot(
            masked_grads.reshape(count_n * row_total, col_total),
            right_factor,
            preferred_element_type=jnp.float32,
        )
        .astype(jnp.bfloat16)
        .reshape(count_n, row_total, col_total)
    )
    rotated = jnp.einsum(
        "ba,nbc->nac", left_masked, rotated_right, preferred_element_type=jnp.float32
    )
    eig_float = eig_block.astype(jnp.float32)
    damping = (
        0.1
        * jnp.sum(eig_float * row_mask[:, None])
        / jnp.maximum(live_rows * col_total, 1).astype(jnp.float32)
    )
    scaled = (rotated / (eig_float + damping)).astype(jnp.bfloat16)
    back_right = (
        jnp.dot(
            scaled.reshape(count_n * row_total, col_total),
            right_factor.T,
            preferred_element_type=jnp.float32,
        )
        .astype(jnp.bfloat16)
        .reshape(count_n, row_total, col_total)
    )
    return jnp.einsum(
        "ab,nbc->nac", left_masked, back_right, preferred_element_type=jnp.float32
    ).astype(jnp.bfloat16)


def precondition_slots(grads, left_all, right_all, eig_all, rows_all):
    slot_count = grads.shape[1]

    def slot_turn(slot_index, output):
        grad_slot = lax.dynamic_index_in_dim(grads, slot_index, 1, keepdims=False)
        live_rows = rows_all[slot_index]
        result = lax.cond(
            live_rows > 0,
            lambda: precondition(
                grad_slot,
                left_all[slot_index],
                right_all[slot_index],
                eig_all[slot_index],
                live_rows,
            ),
            lambda: jnp.zeros(grad_slot.shape, jnp.bfloat16),
        )
        return lax.dynamic_update_index_in_dim(output, result, slot_index, 1)

    return lax.fori_loop(0, slot_count, slot_turn, jnp.zeros(grads.shape, jnp.bfloat16))


def score_block(left_rows, right_rows):
    return lax.dot_general(
        left_rows, right_rows, (((1,), (1,)), ((), ())), preferred_element_type=jnp.float32
    )


def on_device(query_grads, train_grads, left_basis, right_basis, eigenvalues, block_rows):
    slot_total = query_grads.shape[1]
    norm_scale = 1.0 / math.sqrt(slot_total * query_grads.shape[2] * query_grads.shape[3])
    per_source = query_grads.shape[0]
    received = lax.all_to_all(query_grads, "mod", split_axis=1, concat_axis=0, tiled=True)
    result = precondition_slots(received, left_basis, right_basis, eigenvalues, block_rows)
    own_half = result.reshape(result.shape[0], -1)
    train_flat = train_grads.reshape(train_grads.shape[0], -1)
    pair_side = lax.axis_index("pair")
    partner = swapped(own_half, "pair", 0)
    own_scores = score_block(own_half, train_flat)
    far_scores = score_block(partner, train_flat)
    low_half = jnp.where(pair_side == 0, own_scores, far_scores)
    high_half = jnp.where(pair_side == 0, far_scores, own_scores)
    block_count = 2 * per_source * lax.axis_size("mod") // (2 * per_source)
    stacked = jnp.stack(
        [
            low_half.reshape(block_count, per_source, -1),
            high_half.reshape(block_count, per_source, -1),
        ],
        1,
    )
    summed = lax.psum_scatter(
        stacked.reshape(2 * per_source * lax.axis_size("mod"), -1),
        "mod",
        scatter_dimension=0,
        tiled=True,
    )
    return summed * norm_scale


def solution(mesh):
    placed = (
        P(("mod", "pair"), None, None, None),
        P("pair", "mod", None, None),
        P("mod", None, None),
        P("mod", None, None),
        P("mod", None, None),
        P("mod"),
    )
    return jax.shard_map(
        on_device, mesh=mesh, in_specs=placed, out_specs=P("mod", "pair"), check_vma=False
    )
```

profile of v0, /device:TPU:0, one launch (start us, length us, event | category | flops | bytes accessed | tf_op | source)
XLA Modules:
  0.0 510.6 jit_solution(12560037033643082083)
XLA Ops:
  6.5 5.5 %copy.19 = bf16[4,256,16,128]{3,2,0,1:T(8,128)(2,1)} copy(bf16[4,256,16,128]{3,2,1,0:T(8,128)(2,1)} %param.10) | data formatting | bytes 8388608 | tf_op args[0]
  12.0 11.8 %all-to-all-start = ((bf16[4,256,16,128]{3,2,0,1:T(8,128)(2,1)}), bf16[4,256,16,128]{3,2,0,1:T(8,128)(2,1)}, u32[]{:S(2)}, u32[]{:S(2)}) async-start(bf16[4,256,16,128]{3,2,0,1:T(8,128)(2,1)} %copy.19), calls=%async_computation | async-start | bytes 8388608 | tf_op jit(solution)/shard_map/all_to_all | solution.py:87
  23.8 0.0 reduce-scatter.2.cloned.1.call-start
  23.8 56.0 %all-to-all-done = bf16[4,256,16,128]{3,2,0,1:T(8,128)(2,1)} async-done(((bf16[4,256,16,128]{3,2,0,1:T(8,128)(2,1)}), bf16[4,256,16,128]{3,2,0,1:T(8,128)(2,1)}, u32[]{:S(2)}, u32[]{:S(2)}) %all-to-all-start) | async-done | bytes 4194336 | tf_op jit(solution)/shard_map/all_to_all | solution.py:87
  79.8 5.4 %copy.20 = bf16[64,4,4,16,128]{4,3,2,1,0:T(8,128)(2,1)} copy(bf16[64,4,4,16,128]{4,3,1,2,0:T(8,128)(2,1)} %bitcast.15) | data formatting | bytes 8388608 | tf_op jit(solution)/shard_map/all_to_all | solution.py:87
  85.2 25.2 %while.13 = (s32[]{:T(128)}, bf16[256,4,16,128]{0,3,2,1:T(8,128)(2,1)}, s32[4]{0:T(128)S(1)}, bf16[256,4,16,128]{3,2,1,0:T(8,128)(2,1)}, bf16[4,128,128]{2,1,0:T...) while((s32[]{:T(128)}, ...), condition=%wide.region_4.5_spmd, body=%wide.region_0.4_spmd.sunk | while | flops 306196512 | bytes 14781425 | solution.py:74
  85.2 0.6 dynamic_slice.45
  86.5 6.2 %conditional.2 = (bf16[256,1,16,128]{3,2,0,1:T(8,128)(2,1)S(1)}) conditional(s32[]{:T(128)} %convert_element_type.116, () %tuple.41, (bf16[256,4,16,128]{3,2,1,0:T(8,128)(2,1)}, s32[]{:T(128)}, s32[]{:T(128)}, bf16[4,128,128]{2,1,0:T(8,128)(2,1)S(1)}, bf16[4,16,16]{2,1,0:T(8,128)(2,1)S(1)}, /*index=5*/bf16[4,16,128]{2,1,0:T(8,128)(2,1)S(1)}) %tuple.42), branch_computations={%region_1.1_spmd, %region_2.3_spmd} | conditional | flops 306196512 | bytes 10586442 | solution.py:61
  86.5 0.6 compare_convert_fusion
  87.1 0.7 fusion.8
  89.2 1.5 multiply_convert_fusion
  90.7 0.4 convolution_convert_fusion.1
  91.2 0.6 fusion
  91.7 0.4 convolution_convert_fusion
  92.2 0.5 fusion.1
  92.6 0.8 copy.42
  93.4 1.0 constant_dynamic-update-slice_fusion.2
  94.5 0.6 dynamic_slice.45
  95.7 6.2 %conditional.2 = (bf16[256,1,16,128]{3,2,0,1:T(8,128)(2,1)S(1)}) conditional(s32[]{:T(128)} %convert_element_type.116, () %tuple.41, (bf16[256,4,16,128]{3,2,1,0:T(8,128)(2,1)}, s32[]{:T(128)}, s32[]{:T(128)}, bf16[4,128,128]{2,1,0:T(8,128)(2,1)S(1)}, bf16[4,16,16]{2,1,0:T(8,128)(2,1)S(1)}, /*index=5*/bf16[4,16,128]{2,1,0:T(8,128)(2,1)S(1)}) %tuple.42), branch_computations={%region_1.1_spmd, %region_2.3_spmd} | conditional | flops 306196512 | bytes 10586442 | solution.py:61
  95.8 0.6 compare_convert_fusion
  96.4 0.7 fusion.8
  98.4 1.5 multiply_convert_fusion
  100.0 0.4 convolution_convert_fusion.1
  100.4 0.6 fusion
  101.0 0.4 convolution_convert_fusion
  101.4 0.5 fusion.1
  101.9 0.8 copy.42
  102.7 1.1 constant_dynamic-update-slice_fusion.2
  103.8 0.6 dynamic_slice.45
  105.0 0.2 conditional.2
  105.1 0.1 broadcast_in_dim.18
  105.2 0.8 copy.42
  106.0 1.1 constant_dynamic-update-slice_fusion.2
  107.1 0.6 dynamic_slice.45
  108.3 0.2 conditional.2
  108.3 0.1 broadcast_in_dim.18
  108.5 0.8 copy.42
  109.3 1.1 constant_dynamic-update-slice_fusion.2
  110.4 13.9 %fusion.19 = f32[256,512]{1,0:T(8,128)S(1)} fusion(bf16[256,4,16,128]{0,3,2,1:T(8,128)(2,1)} %get-tuple-element.173, bf16[512,4,16,128]{3,2,1,0:T(8,128)(2,1)} %param.11), kind=kOutput, calls=%fused_computation.27 | convolution fusion | flops 2147483648 | bytes 13107200 | tf_op jit(solution)/shard_map/dot_general | solution.py:78
  124.3 14.2 %broadcast_select_fusion.1 = (f32[256,512]{1,0:T(8,128)S(1)}, f32[256,512]{1,0:T(8,128)S(1)}) fusion(f32[256,512]{1,0:T(8,128)S(1)} %fusion.19, pred[]{:T(512)S(6)} %eq.4, bf16[256,8192]{0,1:T(8,128)(2,1)} %collective-permute-done, bf16[64,8,64,128]{3,2,1,0:T(8,128)(2,1)} %bitcast.62), kind=kOutput, calls=%fused_computation.30 | convolution fusion | flops 2147745792 | bytes 14155777 | tf_op jit(solution)/shard_map/dot_general | solution.py:78
  138.5 0.1 stack_reshape.6
  138.7 0.1 stack_reshape.7
  138.8 0.2 pad_maximum_fusion
  139.1 0.2 copy.24
  139.2 1.3 reshape.79
  140.6 0.0 reduce-scatter.2.cloned.1.call-update
  140.6 361.8 %reduce-scatter.2.cloned.1.call-done = f32[8,512]{1,0:T(8,128)} async-done(((f32[512,512]{1,0:T(8,128)}), f32[8,512]{1,0:T(8,128)}) %reduce-scatter.2.cloned.1.call-update) | async-done | bytes 16400 | tf_op jit(solution)/shard_map/reduce_scatter | solution.py:105
  502.4 1.3 broadcast_multiply_fusion
  (13 shorter events, 0.0 us)
Async XLA Ops:
  12.0 67.8 %all-to-all-start = ((bf16[4,256,16,128]{3,2,0,1:T(8,128)(2,1)}), bf16[4,256,16,128]{3,2,0,1:T(8,128)(2,1)}, u32[]{:S(2)}, u32[]{:S(2)}) async-start(bf16[4,256,16,128]{3,2,0,1:T(8,128)(2,1)} %copy.19), calls=%async_computation | async-start | bytes 8388608 | tf_op jit(solution)/shard_map/all_to_all | solution.py:87
  23.8 478.6 %reduce-scatter.2.cloned.1.call-start = ((), (), s32[]{:S(2)}) async-start(), calls=%async_computation.2 | async-start | bytes 1064960 | tf_op jit(solution)/shard_map/reduce_scatter | solution.py:105
  79.8 5.4 %copy-start = (bf16[4,128,128]{2,1,0:T(8,128)(2,1)S(1)}, bf16[4,128,128]{2,1,0:T(8,128)(2,1)}, u32[]{:S(2)}) copy-start(bf16[4,128,128]{2,1,0:T(8,128)(2,1)} %param.13) | copy-start | bytes 393220
  79.8 5.4 %copy-start.1 = (bf16[4,16,128]{2,1,0:T(8,128)(2,1)S(1)}, bf16[4,16,128]{2,1,0:T(8,128)(2,1)}, u32[]{:S(2)}) copy-start(bf16[4,16,128]{2,1,0:T(8,128)(2,1)} %param.14) | copy-start | bytes 49156
  79.8 5.4 %copy-start.2 = (bf16[4,16,16]{2,1,0:T(8,128)(2,1)S(1)}, bf16[4,16,16]{2,1,0:T(8,128)(2,1)}, u32[]{:S(2)}) copy-start(bf16[4,16,16]{2,1,0:T(8,128)(2,1)} %param.12) | copy-start | bytes 6148
  79.8 5.4 %copy-start.3 = (s32[4]{0:T(128)S(1)}, s32[4]{0:T(128)}, u32[]{:S(2)}) copy-start(s32[4]{0:T(128)} %param.15) | copy-start | bytes 52
  110.4 13.9 %collective-permute-start = (bf16[256,8192]{0,1:T(8,128)(2,1)}, bf16[256,8192]{0,1:T(8,128)(2,1)}, u32[]{:S(2)}, u32[]{:S(2)}) collective-permute-start(bf16[256,8192]{0,1:T(8,128)(2,1)} %bitcast.63), channel_id=1, source_target_pairs={{0,1},{1,0},{2,3},{3,2},{4,5},{5,4},{6,7},{7,6},{8,9},{9,8},{10,11... | collective-permute-start | bytes 12582920 | tf_op jit(solution)/shard_map/ppermute | solution.py:12
Sparse Core Ops, SparseCore 0:
  140.7 361.6 reduce-scatter.1
where the time goes:
time: 511 us
  waiting for transfers between devices  418 us (82%)
  matrix products  31.9 us (6%)
  local copies, waits for them, and re-layouts  22.8 us (4%)
  between operations  13.5 us (3%)
  starting transfers between devices  11.8 us (2%)
  other arithmetic  7.38 us (1%)
  loops' own time  5.39 us (1%)
    reduce_scatter x1, waiting for transfers between devices, on_device(): lax.psum_scatter(stacked.reshape(2 * per_source * lax.axis_size('mod'), -...  362 us
    all_to_all x1, waiting for transfers between devices, on_device(): lax.all_to_all(query_grads, 'mod', split_axis=1, concat_axis=0, tiled=True)  56 us
    dot_general x2, matrix products, score_block(): lax.dot_general(left_rows, right_rows, (((1,), (1,)), ((), ())), preferre...  28.1 us
    all_to_all x1, starting transfers between devices, on_device(): lax.all_to_all(query_grads, 'mod', split_axis=1, concat_axis=0, tiled=True)  11.8 us
  transfers between devices with their start and end apart: 3, of which 2 were waited for; matrix products, arithmetic and copies ran while one was open for 3% of the time, Pallas kernels for 0%

commit v1 on v0

v1 whole, which is shorter than its diff:
```python
import math

import jax
import jax.numpy as jnp
from jax import lax
from jax.experimental import pallas as pl
from jax.experimental.pallas import tpu as pltpu
from jax.sharding import PartitionSpec as P


GROUP = 16
REFINED = (True, False, True)


def dot(a, b):
    return jnp.dot(a, b, preferred_element_type=jnp.float32)


def dot_by_rows(a, b):
    return lax.dot_general(a, b, (((1,), (1,)), ((), ())), preferred_element_type=jnp.float32)


def halves(value):
    high = value.astype(jnp.bfloat16)
    return high, (value - high.astype(jnp.float32)).astype(jnp.bfloat16)


def mixed_by(matrix, value, refined):
    if not refined:
        return dot(matrix, value.astype(jnp.bfloat16))
    high, low = halves(value)
    return dot(matrix, high) + dot(matrix, low)


def arrange_kernel(in_ref, out_ref, held_ref, in_sem, out_sem):
    queries = range(in_ref.shape[0])
    fetch = [
        pltpu.make_async_copy(in_ref.at[q], held_ref.at[q], in_sem.at[q]) for q in queries
    ]
    place = [
        pltpu.make_async_copy(held_ref.at[q], out_ref.at[:, q], out_sem.at[q]) for q in queries
    ]
    for copy in fetch:
        copy.start()
    for q in queries:
        fetch[q].wait()
        place[q].start()
    for copy in place:
        copy.wait()


def by_owner(query_grads, owners):
    count, slot_total, rows, cols = query_grads.shape
    slots = slot_total // owners
    shape = (count, owners, slots, rows, cols)
    return pl.pallas_call(
        arrange_kernel,
        in_specs=[pl.BlockSpec(memory_space=pl.ANY)],
        out_specs=pl.BlockSpec(memory_space=pl.ANY),
        out_shape=jax.ShapeDtypeStruct((owners, count, slots, rows, cols), query_grads.dtype),
        scratch_shapes=[
            pltpu.VMEM(shape, query_grads.dtype),
            pltpu.SemaphoreType.DMA((count,)),
            pltpu.SemaphoreType.DMA((count,)),
        ],
        name="by_owner",
    )(query_grads.reshape(shape))


def train_kernel(
    live_ref, train_ref, left_ref, right_ref, eig_ref, out_ref, turn_ref, mix_ref, pair_ref, inv_ref
):
    block, rows, cols = train_ref.shape
    span = GROUP * rows
    live = live_ref[pl.program_id(0)]

    @pl.when(live == 0)
    def _():
        out_ref[...] = jnp.zeros_like(out_ref)

    @pl.when(live > 0)
    def _():
        at = lambda shape, axis: lax.broadcasted_iota(jnp.int32, shape, axis)
        square = (rows, rows)
        kept = (at(square, 0) < live) & (at(square, 1) < live)
        left = jnp.where(kept, left_ref[...].astype(jnp.float32), 0.0).astype(jnp.bfloat16)
        tall, big = (span, rows), (span, span)
        ones = lambda mask: mask.astype(jnp.float32).astype(jnp.bfloat16)
        inner = ones(at(tall, 0) % rows == at(tall, 1))
        outer = ones(at(tall, 0) // GROUP == at(tall, 1))
        narrow = lambda value: value.astype(jnp.bfloat16)
        turn = dot_by_rows(narrow(dot_by_rows(inner, left)), inner)
        mix = dot_by_rows(narrow(dot(outer, left)), inner)
        turn_ref[...] = narrow(jnp.where(at(big, 0) // rows == at(big, 1) // rows, turn, 0.0))
        mix_ref[...] = narrow(jnp.where(at(big, 0) % GROUP == at(big, 1) // rows, mix, 0.0))
        right = right_ref[...]
        pair_ref[...] = jnp.zeros_like(pair_ref)
        pair_ref[:cols, :cols] = right
        pair_ref[cols:, cols:] = right
        eig = eig_ref[...].astype(jnp.float32)
        summed = jnp.sum(jnp.where(at(eig.shape, 0) < live, eig, 0.0))
        damping = 0.1 * summed / jnp.maximum(live * cols, 1).astype(jnp.float32)
        inverse = jnp.broadcast_to((1.0 / (eig + damping))[None], (GROUP, rows, cols))
        inverse = inverse.reshape(span, cols)
        inv_ref[...] = jnp.concatenate([inverse, inverse], 1)
        turn, mix, pair, inverse = turn_ref[...], mix_ref[...], pair_ref[...], inv_ref[...]
        for two in range(block // (2 * GROUP)):
            first, second = (
                train_ref[(2 * two + k) * GROUP : (2 * two + k + 1) * GROUP].reshape(span, cols)
                for k in range(2)
            )
            value = dot(jnp.concatenate([first, second], 1), pair)
            value = mixed_by(turn, value, REFINED[0]) * inverse
            if REFINED[1]:
                high, low = halves(value)
                value = dot_by_rows(high, pair) + dot_by_rows(low, pair)
            else:
                value = dot_by_rows(narrow(value), pair)
            value = narrow(mixed_by(mix, value, REFINED[2]))
            for k in range(2):
                base = (2 * two + k) * GROUP
                for row in range(rows):
                    out_ref[base : base + GROUP, row * cols : (row + 1) * cols] = value[
                        row * GROUP : (row + 1) * GROUP, k * cols : (k + 1) * cols
                    ]


def preconditioned_train(live, train_grads, left, right, eigenvalues, part, parts):
    count, slots, rows, cols = train_grads.shape
    block = count // parts
    span = GROUP * rows
    per_slot = lambda *shape: pl.BlockSpec((None, *shape), lambda s, live: (s, 0, 0))
    return pl.pallas_call(
        train_kernel,
        grid_spec=pltpu.PrefetchScalarGridSpec(
            num_scalar_prefetch=1,
            grid=(slots,),
            in_specs=[
                pl.BlockSpec((block, None, rows, cols), lambda s, live: (part, s, 0, 0)),
                per_slot(rows, rows),
                per_slot(cols, cols),
                per_slot(rows, cols),
            ],
            out_specs=pl.BlockSpec((block, rows * cols), lambda s, live: (0, s)),
            scratch_shapes=[
                pltpu.VMEM((span, span), jnp.bfloat16),
                pltpu.VMEM((span, span), jnp.bfloat16),
                pltpu.VMEM((2 * cols, 2 * cols), jnp.bfloat16),
                pltpu.VMEM((span, 2 * cols), jnp.float32),
            ],
        ),
        out_shape=jax.ShapeDtypeStruct((block, slots * rows * cols), jnp.bfloat16),
        cost_estimate=pl.CostEstimate(
            flops=8 * block * slots * rows * cols * span, bytes_accessed=1 << 23, transcendentals=0
        ),
    )(live, train_grads, left, right, eigenvalues)


def score_kernel(side_ref, query_ref, *refs):
    train_refs, (out_ref, sort_ref, flat_ref, sum_ref) = refs[:-4], refs[-4:]
    parts = len(train_refs) // 2
    count, rows, cols = query_ref.shape
    span = GROUP * rows
    step, last = pl.program_id(0), pl.num_programs(0) - 1
    block = train_refs[0].shape[0]

    @pl.when(step == 0)
    def _():
        to = lax.broadcasted_iota(jnp.int32, (span, span), 0)
        of = lax.broadcasted_iota(jnp.int32, (span, span), 1)
        same = (to % GROUP == of // rows) & (to // GROUP == of % rows)
        sort_ref[...] = same.astype(jnp.float32).astype(jnp.bfloat16)

    sort = sort_ref[...]
    for two in range(count // (2 * GROUP)):
        first, second = (
            query_ref[(2 * two + k) * GROUP : (2 * two + k + 1) * GROUP].reshape(span, cols)
            for k in range(2)
        )
        ordered = dot(sort, jnp.concatenate([first, second], 1)).astype(jnp.bfloat16)
        for k in range(2):
            base = (2 * two + k) * GROUP
            for row in range(rows):
                flat_ref[base : base + GROUP, row * cols : (row + 1) * cols] = ordered[
                    row * GROUP : (row + 1) * GROUP, k * cols : (k + 1) * cols
                ]
    flat = flat_ref[...]
    for index, train_ref in enumerate(train_refs):
        part = dot_by_rows(flat, train_ref[...])
        at = (index // parts, slice(None), pl.ds(index % parts * block, block))

        @pl.when(step == 0)
        def _():
            sum_ref[at] = part

        @pl.when(step > 0)
        def _():
            sum_ref[at] += part

    @pl.when(step == last)
    def _():
        side = side_ref[0]
        out_ref[side] = sum_ref[0].astype(out_ref.dtype)
        out_ref[1 - side] = sum_ref[1].astype(out_ref.dtype)


def scores(side, queries, train_parts):
    count, slots, rows, cols = queries.shape
    block = train_parts[0].shape[0]
    train_count = block * len(train_parts) // 2
    span = GROUP * rows
    flat = pl.BlockSpec((block, rows * cols), lambda s, side: (0, s))
    return pl.pallas_call(
        score_kernel,
        grid_spec=pltpu.PrefetchScalarGridSpec(
            num_scalar_prefetch=1,
            grid=(slots,),
            in_specs=[pl.BlockSpec((count, None, rows, cols), lambda s, side: (0, s, 0, 0))]
            + [flat] * len(train_parts),
            out_specs=pl.BlockSpec((2, count, train_count), lambda s, side: (0, 0, 0)),
            scratch_shapes=[
                pltpu.VMEM((span, span), jnp.bfloat16),
                pltpu.VMEM((count, rows * cols), jnp.bfloat16),
                pltpu.VMEM((2, count, train_count), jnp.float32),
            ],
        ),
        out_shape=jax.ShapeDtypeStruct((2, count, train_count), jnp.bfloat16),
        cost_estimate=pl.CostEstimate(
            flops=4 * count * train_count * slots * rows * cols, bytes_accessed=1 << 24, transcendentals=0
        ),
        name="scores",
    )(side, queries, *train_parts)


def on_device(query_grads, train_grads, left_basis, right_basis, eigenvalues, block_rows):
    per_source, slot_total, rows, cols = query_grads.shape
    owners = lax.axis_size("mod")
    slots = slot_total // owners
    norm_scale = 1.0 / math.sqrt(slot_total * rows * cols)

    sent = by_owner(query_grads, owners)
    got = lax.all_to_all(sent, "mod", split_axis=0, concat_axis=0, tiled=True)
    got = got.reshape(owners * per_source, slots, rows, cols)

    parts = 2
    own = [
        preconditioned_train(
            block_rows, train_grads, left_basis, right_basis, eigenvalues, k, parts
        )
        for k in range(parts)
    ]
    far = [lax.ppermute(value, "pair", [(0, 1), (1, 0)]) for value in own]
    side = lax.axis_index("pair").astype(jnp.int32).reshape(1)
    partial = scores(side, got, own + far)
    partial = jnp.swapaxes(partial.reshape(2, owners, per_source, -1), 0, 1)
    partial = partial.reshape(2 * owners, per_source, -1)
    back = lax.all_to_all(partial, ("mod", "pair"), split_axis=0, concat_axis=0, tiled=True)
    back = back.reshape(owners, 2 * per_source, -1)
    return jnp.sum(back.astype(jnp.float32), 0) * norm_scale


def solution(mesh):
    placed = (
        P(("mod", "pair"), None, None, None),
        P("pair", "mod", None, None),
        P("mod", None, None),
        P("mod", None, None),
        P("mod", None, None),
        P("mod"),
    )
    return jax.shard_map(
        on_device, mesh=mesh, in_specs=placed, out_specs=P("mod", "pair"), check_vma=False
    )
```

time: 511 us -> 139 us (0.27)
  waiting for transfers between devices: 418 us -> 54.8 us
  Pallas kernels: 0 us -> 37.2 us
  matrix products: 31.9 us -> 0 us
  local copies, waits for them, and re-layouts: 22.8 us -> 1.42 us
  blocking collectives: 0 us -> 18.6 us
  starting transfers between devices: 11.8 us -> 25.6 us
  between operations: 13.5 us -> 0.04 us
  other arithmetic: 7.38 us -> 0.71 us
  loops' own time: 5.39 us -> 0 us
    reduce_scatter x1 -> x0, waiting for transfers between devices: 362 us -> none  [on_device(): lax.psum_scatter(stacked.reshape(2 * per_source * lax.axis_size('mod'), -...]
    pallas_call x0 -> x4, Pallas kernels: none -> 37.2 us  [the longest x2 17.5 us: preconditioned_train(): pl.pallas_call(train_kernel, grid_spec=pltpu.PrefetchScalarGridSpec(num_s...]
    dot_general x10 -> x0, matrix products: 31.9 us -> none  [the longest x2 28.1 us: score_block(): lax.dot_general(left_rows, right_rows, (((1,), (1,)), ((), ())), preferre...]
    all_to_all x0 -> x1, blocking collectives: none -> 18.6 us  [on_device(): lax.all_to_all(partial, ('mod', 'pair'), split_axis=0, concat_axis=0, til...]
    all_to_all x1, starting transfers between devices: 11.8 us -> 25.1 us  [on_device(): got = lax.all_to_all(sent, 'mod', split_axis=0, concat_axis=0, tiled=True)]
    dynamic_update_slice x8 -> x0, local copies, waits for them, and re-layouts: 7.43 us -> none  [slot_turn(): return lax.dynamic_update_index_in_dim(output, result, slot_index, 1)]
    unnamed x9 -> x0, local copies, waits for them, and re-layouts: 5.47 us -> none
    another operation x5 -> x0, loops' own time: 5.39 us -> none  [the longest x4 2.76 us: slot_turn(): lax.cond(live_rows > 0, lambda: precondition(grad_slot, left_all[slot_ind...]
  transfers between devices with their start and end apart: 3 -> 3, of which waited for: 2 -> 1; matrix products, arithmetic and copies ran while one was open for 3% -> 0% of each run, Pallas kernels for 0% -> 9%
where the time goes in v1:
time: 139 us; the launch traced here: 138 us
  waiting for transfers between devices  54.8 us (39%)
  Pallas kernels  37.2 us (27%)
  starting transfers between devices  25.6 us (18%)
  blocking collectives  18.6 us (13%)
  local copies, waits for them, and re-layouts  1.42 us (1%)
    all_to_all x1, waiting for transfers between devices, on_device(): got = lax.all_to_all(sent, 'mod', split_axis=0, concat_axis=0, tiled=True)  54.8 us
    all_to_all x1, starting transfers between devices, on_device(): got = lax.all_to_all(sent, 'mod', split_axis=0, concat_axis=0, tiled=True)  25.1 us
    all_to_all x1, blocking collectives, on_device(): lax.all_to_all(partial, ('mod', 'pair'), split_axis=0, concat_axis=0, til...  18.6 us
    pallas_call x2, Pallas kernels, preconditioned_train(): pl.pallas_call(train_kernel, grid_spec=pltpu.PrefetchScalarGridSpec(num_s...  17.5 us
    pallas_call x1, Pallas kernels, scores(): pl.pallas_call(score_kernel, grid_spec=pltpu.PrefetchScalarGridSpec(num_s...  16.4 us
    pallas_call x1, Pallas kernels, by_owner(): pl.pallas_call(arrange_kernel, in_specs=[pl.BlockSpec(memory_space=pl.ANY...  3.34 us
  transfers between devices with their start and end apart: 3, of which 1 were waited for; matrix products, arithmetic and copies ran while one was open for 0% of the time, Pallas kernels for 9%

profile of v1, /device:TPU:0, one launch (start us, length us, event | category | flops | bytes accessed | tf_op | source)
XLA Modules:
  0.0 138.4 jit_solution(803973781433812)
XLA Ops:
  0.0 8.7 %shard_map.64.refs_0_ = bf16[256,8192]{1,0:T(8,128)(2,1)} custom-call(s32[4]{0:T(128)} %live_ref.3, bf16[512,4,16,128]{3,2,1,0:T(8,128)(2,1)} %train_ref.3, bf16[4,16,16]{2,1,0:T(8,128)(2,1)} %left_ref.3, bf16[4,128,128]{2,1,0:T(8,128)(2,1)} %right_ref.3, bf16[4,16,128]{2,1,0:T(8,128)(2,1)} %eig_ref.3), custom_call_target="tpu_custom_call" | custom-call | flops 4294967296 | bytes 8388608 | tf_op jit(solution)/shard_map/pallas_call | solution.py:133
  8.7 0.0 collective-permute-start
  8.7 8.7 %shard_map.65.refs_1_ = bf16[256,8192]{1,0:T(8,128)(2,1)} custom-call(s32[4]{0:T(128)} %live_ref.3, bf16[512,4,16,128]{3,2,1,0:T(8,128)(2,1)} %train_ref.3, bf16[4,16,16]{2,1,0:T(8,128)(2,1)} %left_ref.3, bf16[4,128,128]{2,1,0:T(8,128)(2,1)} %right_ref.3, bf16[4,16,128]{2,1,0:T(8,128)(2,1)} %eig_ref.3), custom_call_target="tpu_custom_call" | custom-call | flops 4294967296 | bytes 8388608 | tf_op jit(solution)/shard_map/pallas_call | solution.py:133
  17.5 0.5 collective-permute-start.1
  18.0 3.3 %by_owner.1 = bf16[64,4,4,16,128]{4,3,2,1,0:T(8,128)(2,1)} custom-call(bf16[4,64,4,16,128]{4,3,2,1,0:T(8,128)(2,1)} %bitcast.6), custom_call_target="tpu_custom_call" | custom-call | tf_op jit(solution)/shard_map/by_owner/pallas_call | solution.py:56
  21.3 25.1 %all-to-all-start = ((bf16[64,4,4,16,128]{4,3,2,1,0:T(8,128)(2,1)}), bf16[64,4,4,16,128]{4,3,2,1,0:T(8,128)(2,1)}, u32[]{:S(2)}, u32[]{:S(2)}) async-start(bf16[64,4,4,16,128]{4,3,2,1,0:T(8,128)(2,1)} %by_owner.1), calls=%async_computation | async-start | bytes 8388608 | tf_op jit(solution)/shard_map/all_to_all | solution.py:242
  46.5 54.8 %all-to-all-done = bf16[64,4,4,16,128]{4,3,2,1,0:T(8,128)(2,1)} async-done(((bf16[64,4,4,16,128]{4,3,2,1,0:T(8,128)(2,1)}), bf16[64,4,4,16,128]{4,3,2,1,0:T(8,128)(2,1)}, u32[]{:S(2)}, u32[]{:S(2)}) %all-to-all-start) | async-done | bytes 4194336 | tf_op jit(solution)/shard_map/all_to_all | solution.py:242
  101.3 0.0 collective-permute-done.refs_2_
  101.3 0.0 collective-permute-done.1.refs_3_
  101.3 16.4 %scores.1 = bf16[2,256,512]{2,1,0:T(8,128)(2,1)} custom-call(s32[1]{0:T(128)} %bitcast.side_ref, bf16[256,4,16,128]{3,2,1,0:T(8,128)(2,1)} %bitcast.2.query_ref, bf16[256,8192]{1,0:T(8,128)(2,1)} %shard_map.64.refs_0_, bf16[256,8192]{1,0:T(8,128)(2,1)} %shard_map.65.refs_1_, bf16[256,8192]{1,0:T(8,128)(2,1)} %collective-permute-done.refs_2_, ...), custom_call_target="tpu_custom_call" | custom-call | flops 4294967296 | bytes 16777216 | tf_op jit(solution)/shard_map/scores/pallas_call | solution.py:213
  117.7 1.2 reshape.21
  118.9 0.2 copy.7
  119.1 18.6 %all_to_all.10 = bf16[128,4,512]{2,1,0:T(4,128)(2,1)S(1)} all-to-all(bf16[128,4,512]{2,1,0:T(4,128)(2,1)S(1)} %bitcast.7), channel_id=1, replica_groups=mesh['mod'=64,'pair'=2] {'mod','pair'}, dimensions={0} | all-to-all | bytes 1048576 | tf_op jit(solution)/shard_map/all_to_all | solution.py:257
  137.6 0.1 reshape.23
  137.7 0.1 reduce_sum.9
  137.8 0.6 broadcast_multiply_fusion
Async XLA Ops:
  8.7 92.6 %collective-permute-start = (bf16[256,8192]{1,0:T(8,128)(2,1)}, bf16[256,8192]{1,0:T(8,128)(2,1)}, u32[]{:S(2)}, u32[]{:S(2)}) collective-permute-start(bf16[256,8192]{1,0:T(8,128)(2,1)} %shard_map.64.refs_0_), channel_id=1, source_target_pairs={{0,1},{1,0},{2,3},{3,2},{4,5},{5,4},{6,7},{7,6},{8,9},{9,8},{10,11... | collective-permute-start | bytes 12582920 | tf_op jit(solution)/shard_map/ppermute | solution.py:252
  17.5 83.8 %collective-permute-start.1 = (bf16[256,8192]{1,0:T(8,128)(2,1)}, bf16[256,8192]{1,0:T(8,128)(2,1)}, u32[]{:S(2)}, u32[]{:S(2)}) collective-permute-start(bf16[256,8192]{1,0:T(8,128)(2,1)} %shard_map.65.refs_1_), channel_id=1, source_target_pairs={{0,1},{1,0},{2,3},{3,2},{4,5},{5,4},{6,7},{7,6},{8,9},{9,8},{10,11... | collective-permute-start | bytes 12582920 | tf_op jit(solution)/shard_map/ppermute | solution.py:252
  21.3 80.0 %all-to-all-start = ((bf16[64,4,4,16,128]{4,3,2,1,0:T(8,128)(2,1)}), bf16[64,4,4,16,128]{4,3,2,1,0:T(8,128)(2,1)}, u32[]{:S(2)}, u32[]{:S(2)}) async-start(bf16[64,4,4,16,128]{4,3,2,1,0:T(8,128)(2,1)} %by_owner.1), calls=%async_computation | async-start | bytes 8388608 | tf_op jit(solution)/shard_map/all_to_all | solution.py:242

commit v2 on v1

v2 whole, which is shorter than its diff:
```python
import functools
import math

import jax
import jax.numpy as jnp
from jax import lax
from jax.experimental import pallas as pl
from jax.experimental.pallas import tpu as pltpu
from jax.sharding import PartitionSpec as P


GROUP = 16
REFINED = (True, False, True)


def dot(a, b):
    return jnp.dot(a, b, preferred_element_type=jnp.float32)


def dot_by_rows(a, b):
    return lax.dot_general(a, b, (((1,), (1,)), ((), ())), preferred_element_type=jnp.float32)


def halves(value):
    high = value.astype(jnp.bfloat16)
    return high, (value - high.astype(jnp.float32)).astype(jnp.bfloat16)


def mixed_by(matrix, value, refined):
    if not refined:
        return dot(matrix, value.astype(jnp.bfloat16))
    high, low = halves(value)
    return dot(matrix, high) + dot(matrix, low)


def arrange_kernel(in_ref, out_ref, held_ref, in_sem, out_sem):
    queries = range(in_ref.shape[0])
    fetch = [
        pltpu.make_async_copy(in_ref.at[q], held_ref.at[q], in_sem.at[q]) for q in queries
    ]
    place = [
        pltpu.make_async_copy(held_ref.at[q], out_ref.at[:, q], out_sem.at[q]) for q in queries
    ]
    for copy in fetch:
        copy.start()
    for q in queries:
        fetch[q].wait()
        place[q].start()
    for copy in place:
        copy.wait()


def by_owner(query_grads, owners):
    count, slot_total, rows, cols = query_grads.shape
    slots = slot_total // owners
    shape = (count, owners, slots, rows, cols)
    return pl.pallas_call(
        arrange_kernel,
        in_specs=[pl.BlockSpec(memory_space=pl.ANY)],
        out_specs=pl.BlockSpec(memory_space=pl.ANY),
        out_shape=jax.ShapeDtypeStruct((owners, count, slots, rows, cols), query_grads.dtype),
        scratch_shapes=[
            pltpu.VMEM(shape, query_grads.dtype),
            pltpu.SemaphoreType.DMA((count,)),
            pltpu.SemaphoreType.DMA((count,)),
        ],
        name="by_owner",
    )(query_grads.reshape(shape))


def train_kernel(
    live_ref, train_ref, left_ref, right_ref, eig_ref, out_ref, turn_ref, mix_ref, pair_ref, inv_ref,
    *, first_slot
):
    block, rows, cols = train_ref.shape
    span = GROUP * rows
    live = live_ref[first_slot + pl.program_id(0)]

    @pl.when(live == 0)
    def _():
        out_ref[...] = jnp.zeros_like(out_ref)

    @pl.when((live > 0) & (pl.program_id(1) == 0))
    def _():
        at = lambda shape, axis: lax.broadcasted_iota(jnp.int32, shape, axis)
        square = (rows, rows)
        kept = (at(square, 0) < live) & (at(square, 1) < live)
        left = jnp.where(kept, left_ref[...].astype(jnp.float32), 0.0).astype(jnp.bfloat16)
        tall, big = (span, rows), (span, span)
        ones = lambda mask: mask.astype(jnp.float32).astype(jnp.bfloat16)
        inner = ones(at(tall, 0) % rows == at(tall, 1))
        outer = ones(at(tall, 0) // GROUP == at(tall, 1))
        narrow = lambda value: value.astype(jnp.bfloat16)
        turn = dot_by_rows(narrow(dot_by_rows(inner, left)), inner)
        mix = dot_by_rows(narrow(dot(outer, left)), inner)
        turn_ref[...] = narrow(jnp.where(at(big, 0) // rows == at(big, 1) // rows, turn, 0.0))
        mix_ref[...] = narrow(jnp.where(at(big, 0) % GROUP == at(big, 1) // rows, mix, 0.0))
        right = right_ref[...]
        pair_ref[...] = jnp.zeros_like(pair_ref)
        pair_ref[:cols, :cols] = right
        pair_ref[cols:, cols:] = right
        eig = eig_ref[...].astype(jnp.float32)
        summed = jnp.sum(jnp.where(at(eig.shape, 0) < live, eig, 0.0))
        damping = 0.1 * summed / jnp.maximum(live * cols, 1).astype(jnp.float32)
        inverse = jnp.broadcast_to((1.0 / (eig + damping))[None], (GROUP, rows, cols))
        inverse = inverse.reshape(span, cols)
        inv_ref[...] = jnp.concatenate([inverse, inverse], 1)

    @pl.when(live > 0)
    def _():
        turn, mix, pair, inverse = turn_ref[...], mix_ref[...], pair_ref[...], inv_ref[...]
        for two in range(block // (2 * GROUP)):
            first, second = (
                train_ref[(2 * two + k) * GROUP : (2 * two + k + 1) * GROUP].reshape(span, cols)
                for k in range(2)
            )
            value = dot(jnp.concatenate([first, second], 1), pair)
            value = mixed_by(turn, value, REFINED[0]) * inverse
            if REFINED[1]:
                high, low = halves(value)
                value = dot_by_rows(high, pair) + dot_by_rows(low, pair)
            else:
                value = dot_by_rows(value.astype(jnp.bfloat16), pair)
            value = mixed_by(mix, value, REFINED[2]).astype(jnp.bfloat16)
            for k in range(2):
                base = (2 * two + k) * GROUP
                for row in range(rows):
                    out_ref[base : base + GROUP, row * cols : (row + 1) * cols] = value[
                        row * GROUP : (row + 1) * GROUP, k * cols : (k + 1) * cols
                    ]


def preconditioned_train(live, train_grads, left, right, eigenvalues, part, parts, block):
    count, slots, rows, cols = train_grads.shape
    here = slots // parts
    span = GROUP * rows
    per_slot = lambda *shape: pl.BlockSpec((None, *shape), lambda s, i, live: (part * here + s, 0, 0))
    return pl.pallas_call(
        functools.partial(train_kernel, first_slot=part * here),
        grid_spec=pltpu.PrefetchScalarGridSpec(
            num_scalar_prefetch=1,
            grid=(here, count // block),
            in_specs=[
                pl.BlockSpec((block, None, rows, cols), lambda s, i, live: (i, part * here + s, 0, 0)),
                per_slot(rows, rows),
                per_slot(cols, cols),
                per_slot(rows, cols),
            ],
            out_specs=pl.BlockSpec((block, rows * cols), lambda s, i, live: (i, s)),
            scratch_shapes=[
                pltpu.VMEM((span, span), jnp.bfloat16),
                pltpu.VMEM((span, span), jnp.bfloat16),
                pltpu.VMEM((2 * cols, 2 * cols), jnp.bfloat16),
                pltpu.VMEM((span, 2 * cols), jnp.float32),
            ],
        ),
        out_shape=jax.ShapeDtypeStruct((count, here * rows * cols), jnp.bfloat16),
        cost_estimate=pl.CostEstimate(
            flops=8 * count * here * rows * cols * span, bytes_accessed=1 << 23, transcendentals=0
        ),
    )(live, train_grads, left, right, eigenvalues)


def score_kernel(side_ref, query_ref, *refs, slots_per_part):
    train_refs, refs = refs[:-7], refs[-7:]
    out_ref, query_buf, train_buf, flat_ref, sum_ref, query_sem, train_sem = refs
    slots, count, rows, cols = query_buf.shape
    width = rows * cols
    pieces = 2
    block = train_buf.shape[2]

    def query_copy(slot):
        return pltpu.make_async_copy(
            query_ref.at[:, slot], query_buf.at[slot], query_sem.at[slot]
        )

    def train_copy(slot, piece):
        part, place = divmod(slot, slots_per_part)
        source = train_refs[piece * (len(train_refs) // pieces) + part]
        return pltpu.make_async_copy(
            source.at[:, pl.ds(place * width, width)],
            train_buf.at[slot, piece],
            train_sem.at[slot, piece],
        )

    def fetch(slot):
        query_copy(slot).start()
        for piece in range(pieces):
            train_copy(slot, piece).start()

    fetch(0)
    for slot in range(slots):
        query_copy(slot).wait()
        if slot + 1 < slots:
            fetch(slot + 1)
        for group in range(count // GROUP):
            base = group * GROUP
            ordered = jnp.swapaxes(query_buf[slot, base : base + GROUP], 0, 1)
            for row in range(rows):
                flat_ref[slot % 2, base : base + GROUP, row * cols : (row + 1) * cols] = ordered[row]
        for piece in range(pieces):
            train_copy(slot, piece).wait()
            part = dot_by_rows(flat_ref[slot % 2], train_buf[slot, piece])
            if slot == 0:
                sum_ref[piece] = part
            else:
                sum_ref[piece] += part
    side = side_ref[0]
    lower = lax.broadcasted_iota(jnp.int32, (count, cols), 0) % 8 < 4
    for piece in range(pieces):
        even, odd = [], []
        for pair in range(block // (2 * cols)):
            a = sum_ref[piece, :, 2 * pair * cols : (2 * pair + 1) * cols]
            b = sum_ref[piece, :, (2 * pair + 1) * cols : (2 * pair + 2) * cols]
            even.append(jnp.where(lower, a, pltpu.roll(b, 4, 0)).reshape(count // 8, 8, cols))
            odd.append(jnp.where(lower, pltpu.roll(a, count - 4, 0), b).reshape(count // 8, 8, cols))
        place = side if piece == 0 else 1 - side
        out_ref[:, 0, place] = jnp.concatenate(even, 1).astype(out_ref.dtype)
        out_ref[:, 1, place] = jnp.concatenate(odd, 1).astype(out_ref.dtype)


def scores(side, queries, train_parts):
    count, slots, rows, cols = queries.shape
    block = train_parts[0].shape[0]
    width = rows * cols
    whole = pl.BlockSpec(memory_space=pltpu.HBM)
    out = jax.ShapeDtypeStruct((count // 8, 2, 2, 4 * block // cols, cols), jnp.bfloat16)
    return pl.pallas_call(
        functools.partial(score_kernel, slots_per_part=2 * slots // len(train_parts)),
        in_specs=[pl.BlockSpec(memory_space=pltpu.SMEM)] + [whole] * (1 + len(train_parts)),
        out_shape=out,
        scratch_shapes=[
            pltpu.VMEM((slots, count, rows, cols), jnp.bfloat16),
            pltpu.VMEM((slots, 2, block, width), jnp.bfloat16),
            pltpu.VMEM((2, count, width), jnp.bfloat16),
            pltpu.VMEM((2, count, block), jnp.float32),
            pltpu.SemaphoreType.DMA((slots,)),
            pltpu.SemaphoreType.DMA((slots, 2)),
        ],
        cost_estimate=pl.CostEstimate(
            flops=4 * count * block * slots * width, bytes_accessed=1 << 24, transcendentals=0
        ),
        compiler_params=pltpu.CompilerParams(vmem_limit_bytes=50 << 20),
        name="scores",
    )(side, queries, *train_parts)


def total_kernel(part_ref, out_ref, *, scale):
    summed = jnp.sum(part_ref[...].astype(jnp.float32), 0) * scale
    sides, height, cols = summed.shape
    for side in range(sides):
        for tile in range(height // 4):
            out_ref[side * 4 : side * 4 + 4, tile * cols : (tile + 1) * cols] = summed[
                side, tile * 4 : tile * 4 + 4
            ]


def total(parts, scale):
    _, sides, height, cols = parts.shape
    return pl.pallas_call(
        functools.partial(total_kernel, scale=scale),
        out_shape=jax.ShapeDtypeStruct((4 * sides, height // 4 * cols), jnp.float32),
        compiler_params=pltpu.CompilerParams(vmem_limit_bytes=4 << 20),
        name="total",
    )(parts)


def on_device(query_grads, train_grads, left_basis, right_basis, eigenvalues, block_rows):
    per_source, slot_total, rows, cols = query_grads.shape
    owners = lax.axis_size("mod")
    slots = slot_total // owners
    norm_scale = 1.0 / math.sqrt(slot_total * rows * cols)

    sent = by_owner(query_grads, owners)
    got = lax.all_to_all(sent, "mod", split_axis=0, concat_axis=0, tiled=True)
    got = got.reshape(owners * per_source, slots, rows, cols)

    parts = 2
    own = [
        preconditioned_train(
            block_rows, train_grads, left_basis, right_basis, eigenvalues, k, parts, 256
        )
        for k in range(parts)
    ]
    far = [lax.ppermute(value, "pair", [(0, 1), (1, 0)]) for value in own]
    side = lax.axis_index("pair").astype(jnp.int32).reshape(1)
    partial = scores(side, got, own + far)
    partial = partial.reshape(2 * owners, *partial.shape[3:])
    back = lax.all_to_all(partial, ("mod", "pair"), split_axis=0, concat_axis=0, tiled=True)
    return total(back.reshape(owners, 2, *back.shape[1:]), norm_scale)


def solution(mesh):
    placed = (
        P(("mod", "pair"), None, None, None),
        P("pair", "mod", None, None),
        P("mod", None, None),
        P("mod", None, None),
        P("mod", None, None),
        P("mod"),
    )
    return jax.shard_map(
        on_device, mesh=mesh, in_specs=placed, out_specs=P("mod", "pair"), check_vma=False
    )
```

time: 139 us -> 132 us (0.950)
  Pallas kernels: 37.2 us -> 30.5 us
  starting transfers between devices: 25.6 us -> 27.1 us
  local copies, waits for them, and re-layouts: 1.42 us -> 0 us
    pallas_call x3 -> x4, Pallas kernels: 33.9 us -> 27.2 us  [the longest x2 17.5 us: preconditioned_train(): pl.pallas_call(functools.partial(train_kernel, first_slot=part * here), g...]
    all_to_all x1, starting transfers between devices: 25.1 us -> 26.5 us  [on_device(): got = lax.all_to_all(sent, 'mod', split_axis=0, concat_axis=0, tiled=True)]
  transfers between devices with their start and end apart: 3 -> 3, of which waited for: 1 -> 1; matrix products, arithmetic and copies ran while one was open for 0% -> 0% of each run, Pallas kernels for 9% -> 7%
where the time goes in v2:
time: 132 us; the launch traced here: 131 us
  waiting for transfers between devices  54.7 us (41%)
  Pallas kernels  30.5 us (23%)
  starting transfers between devices  27.1 us (21%)
  blocking collectives  18.6 us (14%)
    all_to_all x1, waiting for transfers between devices, on_device(): got = lax.all_to_all(sent, 'mod', split_axis=0, concat_axis=0, tiled=True)  54.6 us
    all_to_all x1, starting transfers between devices, on_device(): got = lax.all_to_all(sent, 'mod', split_axis=0, concat_axis=0, tiled=True)  26.5 us
    all_to_all x1, blocking collectives, on_device(): lax.all_to_all(partial, ('mod', 'pair'), split_axis=0, concat_axis=0, til...  18.6 us
    pallas_call x2, Pallas kernels, preconditioned_train(): pl.pallas_call(functools.partial(train_kernel, first_slot=part * here), g...  17.5 us
    pallas_call x1, Pallas kernels, scores(): pl.pallas_call(functools.partial(score_kernel, slots_per_part=2 * slots /...  8.94 us
    pallas_call x1, Pallas kernels, by_owner(): pl.pallas_call(arrange_kernel, in_specs=[pl.BlockSpec(memory_space=pl.ANY...  3.32 us
  transfers between devices with their start and end apart: 3, of which 1 were waited for; matrix products, arithmetic and copies ran while one was open for 0% of the time, Pallas kernels for 7%

profile of v2, /device:TPU:0, one launch (start us, length us, event | category | flops | bytes accessed | tf_op | source)
XLA Modules:
  0.0 130.9 jit_solution(5279655966910456363)
XLA Ops:
  0.0 12.0 %shard_map.64.refs_0_ = bf16[512,4096]{1,0:T(8,128)(2,1)} custom-call(s32[4]{0:T(128)} %live_ref.3, bf16[512,4,16,128]{3,2,1,0:T(8,128)(2,1)} %train_ref.3, bf16[4,16,16]{2,1,0:T(8,128)(2,1)} %left_ref.3, bf16[4,128,128]{2,1,0:T(8,128)(2,1)} %right_ref.3, bf16[4,16,128]{2,1,0:T(8,128)(2,1)} %eig_ref.3), custom_call_target="tpu_custom_call" | custom-call | flops 4294967296 | bytes 8388608 | tf_op jit(solution)/shard_map/pallas_call | solution.py:138
  12.0 0.0 collective-permute-start
  12.0 5.6 %shard_map.65.refs_1_ = bf16[512,4096]{1,0:T(8,128)(2,1)} custom-call(s32[4]{0:T(128)} %live_ref.3, bf16[512,4,16,128]{3,2,1,0:T(8,128)(2,1)} %train_ref.3, bf16[4,16,16]{2,1,0:T(8,128)(2,1)} %left_ref.3, bf16[4,128,128]{2,1,0:T(8,128)(2,1)} %right_ref.3, bf16[4,16,128]{2,1,0:T(8,128)(2,1)} %eig_ref.3), custom_call_target="tpu_custom_call" | custom-call | flops 4294967296 | bytes 8388608 | tf_op jit(solution)/shard_map/pallas_call | solution.py:138
  17.5 0.5 collective-permute-start.1
  18.1 3.3 %by_owner.1 = bf16[64,4,4,16,128]{4,3,2,1,0:T(8,128)(2,1)} custom-call(bf16[4,64,4,16,128]{4,3,2,1,0:T(8,128)(2,1)} %bitcast.7), custom_call_target="tpu_custom_call" | custom-call | tf_op jit(solution)/shard_map/by_owner/pallas_call | solution.py:57
  21.4 26.5 %all-to-all-start = ((bf16[64,4,4,16,128]{4,3,2,1,0:T(8,128)(2,1)}), bf16[64,4,4,16,128]{4,3,2,1,0:T(8,128)(2,1)}, u32[]{:S(2)}, u32[]{:S(2)}) async-start(bf16[64,4,4,16,128]{4,3,2,1,0:T(8,128)(2,1)} %by_owner.1), calls=%async_computation | async-start | bytes 8388608 | tf_op jit(solution)/shard_map/all_to_all | solution.py:275
  47.9 54.6 %all-to-all-done = bf16[64,4,4,16,128]{4,3,2,1,0:T(8,128)(2,1)} async-done(((bf16[64,4,4,16,128]{4,3,2,1,0:T(8,128)(2,1)}), bf16[64,4,4,16,128]{4,3,2,1,0:T(8,128)(2,1)}, u32[]{:S(2)}, u32[]{:S(2)}) %all-to-all-start) | async-done | bytes 4194336 | tf_op jit(solution)/shard_map/all_to_all | solution.py:275
  102.6 0.0 collective-permute-done.refs_2_
  102.6 0.0 collective-permute-done.1.refs_3_
  102.6 8.9 %scores.1 = bf16[32,2,2,16,128]{4,3,2,1,0:T(8,128)(2,1)S(1)} custom-call(s32[1]{0:T(128)} %bitcast.side_ref, bf16[256,4,16,128]{3,2,1,0:T(8,128)(2,1)} %bitcast.2.query_ref, bf16[512,4096]{1,0:T(8,128)(2,1)} %shard_map.64.refs_0_, bf16[512,4096]{1,0:T(8,128)(2,1)} %shard_map.65.refs_1_, bf16[512,4096]{1,0:T(8,128)(2,1)} %collective-permute-done.refs_2_, ...), custom_call_target="tpu_custom_call" | custom-call | flops 4294967296 | bytes 16777216 | tf_op jit(solution)/shard_map/scores/pallas_call | solution.py:228
  111.5 18.6 %all_to_all.10 = bf16[128,16,128]{2,1,0:T(8,128)(2,1)S(1)} all-to-all(bf16[128,16,128]{2,1,0:T(8,128)(2,1)S(1)} %bitcast.5), channel_id=1, replica_groups=mesh['mod'=64,'pair'=2] {'mod','pair'}, dimensions={0} | all-to-all | bytes 1048576 | tf_op jit(solution)/shard_map/all_to_all | solution.py:289
  130.1 0.7 total.1
Async XLA Ops:
  12.0 90.6 %collective-permute-start = (bf16[512,4096]{1,0:T(8,128)(2,1)}, bf16[512,4096]{1,0:T(8,128)(2,1)}, u32[]{:S(2)}, u32[]{:S(2)}) collective-permute-start(bf16[512,4096]{1,0:T(8,128)(2,1)} %shard_map.64.refs_0_), channel_id=1, source_target_pairs={{0,1},{1,0},{2,3},{3,2},{4,5},{5,4},{6,7},{7,6},{8,9},{9,8},{10,11... | collective-permute-start | bytes 12582920 | tf_op jit(solution)/shard_map/ppermute | solution.py:285
  17.5 85.1 %collective-permute-start.1 = (bf16[512,4096]{1,0:T(8,128)(2,1)}, bf16[512,4096]{1,0:T(8,128)(2,1)}, u32[]{:S(2)}, u32[]{:S(2)}) collective-permute-start(bf16[512,4096]{1,0:T(8,128)(2,1)} %shard_map.65.refs_1_), channel_id=1, source_target_pairs={{0,1},{1,0},{2,3},{3,2},{4,5},{5,4},{6,7},{7,6},{8,9},{9,8},{10,11... | collective-permute-start | bytes 12582920 | tf_op jit(solution)/shard_map/ppermute | solution.py:285
  21.4 81.2 %all-to-all-start = ((bf16[64,4,4,16,128]{4,3,2,1,0:T(8,128)(2,1)}), bf16[64,4,4,16,128]{4,3,2,1,0:T(8,128)(2,1)}, u32[]{:S(2)}, u32[]{:S(2)}) async-start(bf16[64,4,4,16,128]{4,3,2,1,0:T(8,128)(2,1)} %by_owner.1), calls=%async_computation | async-start | bytes 8388608 | tf_op jit(solution)/shard_map/all_to_all | solution.py:275

commit v3 on v2

--- a/solution.py
+++ b/solution.py
@@ -189,10 +189,12 @@
             train_copy(slot, piece).start()
 
     fetch(0)
+    fetch(1)
     for slot in range(slots):
         query_copy(slot).wait()
-        if slot + 1 < slots:
-            fetch(slot + 1)
+        if slot == 0:
+            for later in range(2, slots):
+                fetch(later)
         for group in range(count // GROUP):
             base = group * GROUP
             ordered = jnp.swapaxes(query_buf[slot, base : base + GROUP], 0, 1)
@@ -275,7 +277,7 @@
     got = lax.all_to_all(sent, "mod", split_axis=0, concat_axis=0, tiled=True)
     got = got.reshape(owners * per_source, slots, rows, cols)
 
-    parts = 2
+    parts = 4
     own = [
         preconditioned_train(
             block_rows, train_grads, left_basis, right_basis, eigenvalues, k, parts, 256

time: 132 us -> 98.4 us (0.75)
  waiting for transfers between devices: 54.7 us -> 34.8 us
  starting transfers between devices: 27.1 us -> 12.8 us
  Pallas kernels: 30.5 us -> 32.4 us
    all_to_all x1, waiting for transfers between devices: 54.6 us -> 30.7 us  [on_device(): got = lax.all_to_all(sent, 'mod', split_axis=0, concat_axis=0, tiled=True)]
    all_to_all x1, starting transfers between devices: 26.5 us -> 11.8 us  [on_device(): got = lax.all_to_all(sent, 'mod', split_axis=0, concat_axis=0, tiled=True)]
    ppermute x2 -> x4, waiting for transfers between devices: 0.01 us -> 4.13 us  [on_device(): far = [lax.ppermute(value, 'pair', [(0, 1), (1, 0)]) for value in own]]
    pallas_call x2 -> x4, Pallas kernels: 17.5 us -> 20.2 us  [preconditioned_train(): pl.pallas_call(functools.partial(train_kernel, first_slot=part * here), g...]
  transfers between devices with their start and end apart: 3 -> 5, of which waited for: 1 -> 3; matrix products, arithmetic and copies ran while one was open for 0% -> 0% of each run, Pallas kernels for 7% -> 21%
where the time goes in v3:
time: 98.4 us; the launch traced here: 97.6 us
  waiting for transfers between devices  34.8 us (35%)
  Pallas kernels  32.4 us (33%)
  blocking collectives  17.5 us (18%)
  starting transfers between devices  12.8 us (13%)
    all_to_all x1, waiting for transfers between devices, on_device(): got = lax.all_to_all(sent, 'mod', split_axis=0, concat_axis=0, tiled=True)  30.7 us
    pallas_call x4, Pallas kernels, preconditioned_train(): pl.pallas_call(functools.partial(train_kernel, first_slot=part * here), g...  20.2 us
    all_to_all x1, blocking collectives, on_device(): lax.all_to_all(partial, ('mod', 'pair'), split_axis=0, concat_axis=0, til...  17.5 us
    all_to_all x1, starting transfers between devices, on_device(): got = lax.all_to_all(sent, 'mod', split_axis=0, concat_axis=0, tiled=True)  11.8 us
    pallas_call x1, Pallas kernels, scores(): pl.pallas_call(functools.partial(score_kernel, slots_per_part=2 * slots /...  8.1 us
    ppermute x4, waiting for transfers between devices, on_device(): far = [lax.ppermute(value, 'pair', [(0, 1), (1, 0)]) for value in own]  4.13 us
    pallas_call x1, Pallas kernels, by_owner(): pl.pallas_call(arrange_kernel, in_specs=[pl.BlockSpec(memory_space=pl.ANY...  3.41 us
  transfers between devices with their start and end apart: 5, of which 3 were waited for; matrix products, arithmetic and copies ran while one was open for 0% of the time, Pallas kernels for 21%

profile of v3, /device:TPU:0, one launch (start us, length us, event | category | flops | bytes accessed | tf_op | source)
XLA Modules:
  0.0 97.6 jit_solution(4428410858695292721)
XLA Ops:
  0.0 3.4 %by_owner.1 = bf16[64,4,4,16,128]{4,3,2,1,0:T(8,128)(2,1)} custom-call(bf16[4,64,4,16,128]{4,3,2,1,0:T(8,128)(2,1)} %bitcast.7), custom_call_target="tpu_custom_call" | custom-call | tf_op jit(solution)/shard_map/by_owner/pallas_call | solution.py:57
  3.4 11.8 %all-to-all-start = ((bf16[64,4,4,16,128]{4,3,2,1,0:T(8,128)(2,1)}), bf16[64,4,4,16,128]{4,3,2,1,0:T(8,128)(2,1)}, u32[]{:S(2)}, u32[]{:S(2)}) async-start(bf16[64,4,4,16,128]{4,3,2,1,0:T(8,128)(2,1)} %by_owner.1), calls=%async_computation | async-start | bytes 8388608 | tf_op jit(solution)/shard_map/all_to_all | solution.py:277
  15.2 9.9 %shard_map.64.refs_0_ = bf16[512,2048]{1,0:T(8,128)(2,1)} custom-call(s32[4]{0:T(128)} %live_ref.7, bf16[512,4,16,128]{3,2,1,0:T(8,128)(2,1)} %train_ref.7, bf16[4,16,16]{2,1,0:T(8,128)(2,1)} %left_ref.7, bf16[4,128,128]{2,1,0:T(8,128)(2,1)} %right_ref.7, bf16[4,16,128]{2,1,0:T(8,128)(2,1)} %eig_ref.7), custom_call_target="tpu_custom_call" | custom-call | flops 2147483648 | bytes 8388608 | tf_op jit(solution)/shard_map/pallas_call | solution.py:138
  25.1 0.0 collective-permute-start
  25.1 3.4 %shard_map.65.refs_1_ = bf16[512,2048]{1,0:T(8,128)(2,1)} custom-call(s32[4]{0:T(128)} %live_ref.7, bf16[512,4,16,128]{3,2,1,0:T(8,128)(2,1)} %train_ref.7, bf16[4,16,16]{2,1,0:T(8,128)(2,1)} %left_ref.7, bf16[4,128,128]{2,1,0:T(8,128)(2,1)} %right_ref.7, bf16[4,16,128]{2,1,0:T(8,128)(2,1)} %eig_ref.7), custom_call_target="tpu_custom_call" | custom-call | flops 2147483648 | bytes 8388608 | tf_op jit(solution)/shard_map/pallas_call | solution.py:138
  28.5 0.5 collective-permute-start.1
  29.0 3.4 %shard_map.66.refs_2_ = bf16[512,2048]{1,0:T(8,128)(2,1)} custom-call(s32[4]{0:T(128)} %live_ref.7, bf16[512,4,16,128]{3,2,1,0:T(8,128)(2,1)} %train_ref.7, bf16[4,16,16]{2,1,0:T(8,128)(2,1)} %left_ref.7, bf16[4,128,128]{2,1,0:T(8,128)(2,1)} %right_ref.7, bf16[4,16,128]{2,1,0:T(8,128)(2,1)} %eig_ref.7), custom_call_target="tpu_custom_call" | custom-call | flops 2147483648 | bytes 8388608 | tf_op jit(solution)/shard_map/pallas_call | solution.py:138
  32.4 0.0 copy-start
  32.4 0.0 collective-permute-start.2
  32.4 3.5 %shard_map.67.refs_3_ = bf16[512,2048]{1,0:T(8,128)(2,1)} custom-call(s32[4]{0:T(128)} %live_ref.7, bf16[512,4,16,128]{3,2,1,0:T(8,128)(2,1)} %train_ref.7, bf16[4,16,16]{2,1,0:T(8,128)(2,1)} %left_ref.7, bf16[4,128,128]{2,1,0:T(8,128)(2,1)} %right_ref.7, bf16[4,16,128]{2,1,0:T(8,128)(2,1)} %eig_ref.7), custom_call_target="tpu_custom_call" | custom-call | flops 2147483648 | bytes 8388608 | tf_op jit(solution)/shard_map/pallas_call | solution.py:138
  35.9 0.5 collective-permute-start.3
  36.4 0.0 collective-permute-done.refs_4_
  36.4 0.0 collective-permute-done.1.refs_5_
  36.4 0.5 collective-permute-done.2.refs_6_
  36.9 3.7 %collective-permute-done.3.refs_7_ = bf16[512,2048]{1,0:T(8,128)(2,1)} collective-permute-done((bf16[512,2048]{1,0:T(8,128)(2,1)}, bf16[512,2048]{1,0:T(8,128)(2,1)}, u32[]{:S(2)}, u32[]{:S(2)}) %collective-permute-start.3) | collective-permute-done | bytes 2097184 | tf_op jit(solution)/shard_map/ppermute | solution.py:287
  40.5 30.7 %all-to-all-done = bf16[64,4,4,16,128]{4,3,2,1,0:T(8,128)(2,1)} async-done(((bf16[64,4,4,16,128]{4,3,2,1,0:T(8,128)(2,1)}), bf16[64,4,4,16,128]{4,3,2,1,0:T(8,128)(2,1)}, u32[]{:S(2)}, u32[]{:S(2)}) %all-to-all-start) | async-done | bytes 4194336 | tf_op jit(solution)/shard_map/all_to_all | solution.py:277
  71.3 0.0 copy-done
  71.3 8.1 %scores.1 = bf16[32,2,2,16,128]{4,3,2,1,0:T(8,128)(2,1)S(1)} custom-call(s32[1]{0:T(128)} %bitcast.side_ref, bf16[256,4,16,128]{3,2,1,0:T(8,128)(2,1)} %bitcast.2.query_ref, bf16[512,2048]{1,0:T(8,128)(2,1)S(1)} %copy-done, bf16[512,2048]{1,0:T(8,128)(2,1)} %shard_map.65.refs_1_, bf16[512,2048]{1,0:T(8,128)(2,1)} %shard_map.66.refs_2_, ...), custom_call_target="tpu_custom_call" | custom-call | flops 4294967296 | bytes 16777216 | tf_op jit(solution)/shard_map/scores/pallas_call | solution.py:230
  79.4 17.5 %all_to_all.10 = bf16[128,16,128]{2,1,0:T(8,128)(2,1)S(1)} all-to-all(bf16[128,16,128]{2,1,0:T(8,128)(2,1)S(1)} %bitcast.5), channel_id=1, replica_groups=mesh['mod'=64,'pair'=2] {'mod','pair'}, dimensions={0} | all-to-all | bytes 1048576 | tf_op jit(solution)/shard_map/all_to_all | solution.py:291
  96.9 0.7 total.1
Async XLA Ops:
  3.4 67.8 %all-to-all-start = ((bf16[64,4,4,16,128]{4,3,2,1,0:T(8,128)(2,1)}), bf16[64,4,4,16,128]{4,3,2,1,0:T(8,128)(2,1)}, u32[]{:S(2)}, u32[]{:S(2)}) async-start(bf16[64,4,4,16,128]{4,3,2,1,0:T(8,128)(2,1)} %by_owner.1), calls=%async_computation | async-start | bytes 8388608 | tf_op jit(solution)/shard_map/all_to_all | solution.py:277
  25.1 11.3 %collective-permute-start = (bf16[512,2048]{1,0:T(8,128)(2,1)}, bf16[512,2048]{1,0:T(8,128)(2,1)}, u32[]{:S(2)}, u32[]{:S(2)}) collective-permute-start(bf16[512,2048]{1,0:T(8,128)(2,1)} %shard_map.64.refs_0_), channel_id=1, source_target_pairs={{0,1},{1,0},{2,3},{3,2},{4,5},{5,4},{6,7},{7,6},{8,9},{9,8},{10,11... | collective-permute-start | bytes 6291464 | tf_op jit(solution)/shard_map/ppermute | solution.py:287
  28.5 7.9 %collective-permute-start.1 = (bf16[512,2048]{1,0:T(8,128)(2,1)}, bf16[512,2048]{1,0:T(8,128)(2,1)}, u32[]{:S(2)}, u32[]{:S(2)}) collective-permute-start(bf16[512,2048]{1,0:T(8,128)(2,1)} %shard_map.65.refs_1_), channel_id=1, source_target_pairs={{0,1},{1,0},{2,3},{3,2},{4,5},{5,4},{6,7},{7,6},{8,9},{9,8},{10,11... | collective-permute-start | bytes 6291464 | tf_op jit(solution)/shard_map/ppermute | solution.py:287
  32.4 38.9 %copy-start = (bf16[512,2048]{1,0:T(8,128)(2,1)S(1)}, bf16[512,2048]{1,0:T(8,128)(2,1)}, u32[]{:S(2)}) copy-start(bf16[512,2048]{1,0:T(8,128)(2,1)} %shard_map.64.refs_0_) | copy-start | bytes 6291460
  32.4 4.5 %collective-permute-start.2 = (bf16[512,2048]{1,0:T(8,128)(2,1)}, bf16[512,2048]{1,0:T(8,128)(2,1)}, u32[]{:S(2)}, u32[]{:S(2)}) collective-permute-start(bf16[512,2048]{1,0:T(8,128)(2,1)} %shard_map.66.refs_2_), channel_id=1, source_target_pairs={{0,1},{1,0},{2,3},{3,2},{4,5},{5,4},{6,7},{7,6},{8,9},{9,8},{10,11... | collective-permute-start | bytes 6291464 | tf_op jit(solution)/shard_map/ppermute | solution.py:287
  35.9 4.6 %collective-permute-start.3 = (bf16[512,2048]{1,0:T(8,128)(2,1)}, bf16[512,2048]{1,0:T(8,128)(2,1)}, u32[]{:S(2)}, u32[]{:S(2)}) collective-permute-start(bf16[512,2048]{1,0:T(8,128)(2,1)} %shard_map.67.refs_3_), channel_id=1, source_target_pairs={{0,1},{1,0},{2,3},{3,2},{4,5},{5,4},{6,7},{7,6},{8,9},{9,8},{10,11... | collective-permute-start | bytes 6291464 | tf_op jit(solution)/shard_map/ppermute | solution.py:287
